TPU v7x, 128 devices: a whole 4x4x4 slice. The times are simulated.
128 devices in a mesh: req: 16 (over x, y_lo, core), head: 8 (over z, y_hi).
Axes of the slice: x: 4, y: 4 (y_hi: 2, y_lo: 2; y = y_hi * 2 + y_lo), z: 4, core: 2. Of those that a mesh axis runs over, the one named last changes fastest.
Arguments:
- tokens: bfloat16 [32768, 2048], P(('req', 'head')), may hold values from -6 to 6
- input_gain: float32 [2048], replicated, may hold values from 0.1 to 1.9
- w_query: bfloat16 [2048, 2048], replicated, may hold values from -0.125 to 0.125
- w_keyval: bfloat16 [2048, 1024], replicated, may hold values from -0.125 to 0.125
- query_gain: float32 [256], replicated, may hold values from 0.1 to 1.9
- key_gain: float32 [256], replicated, may hold values from 0.1 to 1.9
- w_output: bfloat16 [2048, 2048], P('req'), may hold values from -0.125 to 0.125
- laurel_left: bfloat16 [2048, 64], replicated, may hold values from -0.125 to 0.125
- laurel_right: bfloat16 [64, 2048], replicated, may hold values from -0.75 to 0.75
- laurel_gain: float32 [2048], replicated, may hold values from 0.1 to 1.9
- post_gain: float32 [2048], replicated, may hold values from 0.1 to 1.9
- cache_pool: bfloat16 [1024, 64, 1024], P('req'), may hold values from -200 to 200, as said below
- page_table: int32 [64, 16], replicated, may hold values from 0 to 63, as said below
- cached_len: int32 [64], replicated, may hold values from 0 to 1024, as said below
- slot_of: int32 [64], replicated, may hold values from 0 to 63, as said below
Outputs:
- mixed: bfloat16 [32768, 2048], P(('req', 'head'))
Inputs may be any that keep to these rules, and one draw needn't show every extreme that they name: slot_of is a permutation of the 64 requests onto slots. Request i's pages lie in group i // 4. In each group exactly one request is served by the group before it and exactly one by the group after it (group indices cyclic over 16); all others are served by their own group. `page_table`: page p of request i holds its cached positions p*64 to (p+1)*64 - 1; the rows of the 4 requests of one group together name each of that group's 64 pages once. `cached_len`: at least one request that changes group has exactly 1024 cached positions, and some request has none. `cache_pool`: stored keys (already normalized and rotated) and values; entries past a request's cached length are arbitrary.
All inputs are finite; a program needn't handle non-finite values.
Results may differ from a plain program's by a relative error of at most 0.012.
The roundings to bfloat16 on the way count: a program that leaves them out, or rounds other values in their place, can miss the bound.
Values may be sent and summed in bfloat16 or wider, within the bound.
A program may use at most 128 MiB of HBM per device.

v0:
```python
import math

import jax
import jax.numpy as jnp
from jax import lax
from jax.sharding import PartitionSpec as P

NH = 8
KVH = 2
HD = 256
REQ_DEV = 4
CH = 512
PAGE = 64
MAXP = 16


epsilon = 1e-06


def extended_2(block, sides, width):
    for axis, dim in sides:
        count = lax.axis_size(axis)
        forward = [(i, i + 1) for i in range(count - 1)]
        forward.append((count - 1, 0))
        backward = [(target, source) for source, target in forward]
        low = lax.ppermute(
            lax.slice_in_dim(block, block.shape[dim] - width, None, axis=dim), axis, forward
        )
        high = lax.ppermute(lax.slice_in_dim(block, 0, width, axis=dim), axis, backward)
        block = jnp.concatenate([low, block, high], axis=dim)
    return block


def normalize(values_in):
    return values_in * lax.rsqrt(jnp.mean(values_in * values_in, axis=-1, keepdims=True) + epsilon)


def rotate(values_in, position):
    half = values_in.shape[-1] // 2
    exponent = jnp.arange(half, dtype=jnp.float32) * (2.0 / values_in.shape[-1])
    inverse = jnp.power(jnp.float32(1000000.0), -exponent)
    angle = position.astype(jnp.float32)[:, None] * inverse[None, :]
    cosine = jnp.cos(angle)[:, None, :]
    sine = jnp.sin(angle)[:, None, :]
    first_half = values_in[..., :half]
    second_half = values_in[..., half:]
    return jnp.concatenate(
        [first_half * cosine - second_half * sine, second_half * cosine + first_half * sine],
        axis=-1,
    )


def shards(
    tokens,
    input_gain,
    w_query,
    w_keyval,
    query_gain,
    key_gain,
    w_output,
    laurel_left,
    laurel_right,
    laurel_gain,
    post_gain,
    cache_pool,
    page_table,
    cached_len,
    slot_of,
):
    group_count = lax.axis_size("req")
    head_count = lax.axis_size("head")
    group = lax.axis_index("req")
    member = lax.axis_index("head")
    tok_rows = tokens.shape[0]
    total_requests = slot_of.shape[0]
    group_rows = tok_rows * head_count
    per_device = NH // head_count
    per_kv = head_count // KVH
    query_width = per_device * HD
    inputs = tokens.astype(jnp.float32)
    normed = (normalize(inputs) * input_gain).astype(jnp.bfloat16)
    slots = jnp.arange(total_requests, dtype=jnp.int32)
    matches = slot_of[None, :] == slots[:, None]
    request_at = jnp.sum(jnp.where(matches, slots[None, :], 0), axis=1)
    token_rows = group * group_rows + member * tok_rows + jnp.arange(tok_rows, dtype=jnp.int32)
    starts = jnp.take(cached_len, jnp.take(request_at, token_rows // CH))
    position = starts + token_rows % CH
    query_raw = jnp.dot(normed, w_query, preferred_element_type=jnp.float32)
    keyval_raw = jnp.dot(normed, w_keyval, preferred_element_type=jnp.float32)
    query = rotate(normalize(query_raw.reshape(tok_rows, NH, HD)) * query_gain, position).astype(
        jnp.bfloat16
    )
    keyval = keyval_raw.reshape(tok_rows, KVH, 2, HD)
    key = rotate(normalize(keyval[:, :, 0]) * key_gain, position).astype(jnp.bfloat16)
    value = normalize(keyval[:, :, 1]).astype(jnp.bfloat16)
    packed_kv = jnp.concatenate([key, value], axis=-1)
    outgoing = jnp.concatenate([query, jnp.repeat(packed_kv, per_kv, axis=1)], axis=-1)
    incoming = lax.all_to_all(outgoing, "head", split_axis=1, concat_axis=0, tiled=True)[:, 0]
    queries_here = incoming[:, :query_width].reshape(group_rows, per_device, HD)
    fresh_keys = incoming[:, query_width : query_width + HD]
    fresh_values = incoming[:, query_width + HD :]
    low = jnp.dot(normed, laurel_left, preferred_element_type=jnp.float32).astype(jnp.bfloat16)
    laurel = (
        normed.astype(jnp.float32)
        + normalize(jnp.dot(low, laurel_right, preferred_element_type=jnp.float32)) * laurel_gain
    )
    kv_head = member * per_device // (NH // KVH)
    own_start = kv_head * 2 * HD

    def own_channels(block):
        return lax.dynamic_slice_in_dim(block, own_start, 2 * HD, block.ndim - 1)

    target = lax.dynamic_slice_in_dim(slot_of, group * REQ_DEV, REQ_DEV, 0) // REQ_DEV
    local_index = jnp.arange(REQ_DEV, dtype=jnp.int32)
    before = (group + group_count - 1) % group_count
    after = (group + 1) % group_count
    to_before = jnp.sum(jnp.where(target == before, local_index, 0))
    to_after = jnp.sum(jnp.where(target == after, local_index, 0))
    mover_pages = jnp.take(page_table, group * REQ_DEV + jnp.stack([to_before, to_after]), axis=0)
    outbound = jnp.take(cache_pool, mover_pages.reshape(-1), axis=0).reshape(
        2, MAXP, PAGE, 2 * KVH * HD
    )
    extended = extended_2(outbound, (("req", 0),), 1)
    arrived = own_channels(jnp.stack([extended[0], extended[3]]))
    arrived = arrived.reshape(2, MAXP * PAGE, 2 * HD)
    score_scale = HD ** (-0.5)
    cached_rows = MAXP * PAGE

    def one_slot(slot_index):
        request = jnp.take(request_at, group * REQ_DEV + slot_index)
        home_group = request // REQ_DEV
        length = jnp.take(cached_len, request)
        local_pages = jnp.take(page_table, request, axis=0)
        stayed = own_channels(jnp.take(cache_pool, local_pages, axis=0)).reshape(
            cached_rows, 2 * HD
        )
        stored = jnp.where(
            home_group == group, stayed, jnp.where(home_group == before, arrived[0], arrived[1])
        )
        begin = slot_index * CH
        block_queries = lax.dynamic_slice_in_dim(queries_here, begin, CH, 0)
        block_keys = lax.dynamic_slice_in_dim(fresh_keys, begin, CH, 0)
        block_values = lax.dynamic_slice_in_dim(fresh_values, begin, CH, 0)
        cached_scores = (
            jnp.einsum(
                "tnh,kh->ntk", block_queries, stored[:, :HD], preferred_element_type=jnp.float32
            )
            * score_scale
        )
        new_scores = (
            jnp.einsum("tnh,kh->ntk", block_queries, block_keys, preferred_element_type=jnp.float32)
            * score_scale
        )
        visible = (jnp.arange(cached_rows) < length)[None, None, :]
        causal = (jnp.arange(CH)[None, :] <= jnp.arange(CH)[:, None])[None]
        highest = jnp.maximum(
            jnp.max(jnp.where(visible, cached_scores, -jnp.inf), axis=-1),
            jnp.max(jnp.where(causal, new_scores, -jnp.inf), axis=-1),
        )[..., None]
        cached_exp = jnp.where(visible, jnp.exp(cached_scores - highest), 0.0)
        new_exp = jnp.where(causal, jnp.exp(new_scores - highest), 0.0)
        denominator = jnp.sum(cached_exp, axis=-1, keepdims=True) + jnp.sum(
            new_exp, axis=-1, keepdims=True
        )
        cached_weights = (cached_exp / denominator).astype(jnp.bfloat16)
        new_weights = (new_exp / denominator).astype(jnp.bfloat16)
        result = jnp.einsum(
            "ntk,kh->tnh", cached_weights, stored[:, HD:], preferred_element_type=jnp.float32
        )
        result = result + jnp.einsum(
            "ntk,kh->tnh", new_weights, block_values, preferred_element_type=jnp.float32
        )
        return result.astype(jnp.bfloat16).reshape(CH, query_width)

    attended = lax.map(one_slot, jnp.arange(REQ_DEV, dtype=jnp.int32)).reshape(
        group_rows, query_width
    )
    returned = lax.all_to_all(
        attended.reshape(head_count, tok_rows, query_width),
        "head",
        split_axis=0,
        concat_axis=2,
        tiled=True,
    )
    returned = returned.reshape(tok_rows, NH * HD)
    projected = jnp.dot(
        returned,
        lax.all_gather(w_output, "req", axis=0, tiled=True),
        preferred_element_type=jnp.float32,
    )
    attn = normalize(projected) * post_gain
    return ((attn + inputs + laurel) / math.sqrt(2.0)).astype(jnp.bfloat16)


def solution(mesh):
    in_specs = (
        P(("req", "head"), None),
        P(),
        P(),
        P(),
        P(),
        P(),
        P("req", None),
        P(),
        P(),
        P(),
        P(),
        P("req", None, None),
        P(),
        P(),
        P(),
    )
    out_specs = P(("req", "head"), None)
    return jax.shard_map(shards, mesh=mesh, in_specs=in_specs, out_specs=out_specs, check_vma=False)
```

profile of v0, /device:TPU:1, one launch (start us, length us, event | category | flops | bytes accessed | tf_op | source)
XLA Modules:
  0.0 260.2 jit_solution(6800885613458207258)
XLA Ops:
  7.5 1.9 gather_fusion.3
  9.4 1.9 gather_fusion.4
  11.6 3.5 %fusion.45 = f32[256,1024]{1,0:T(8,128)S(1)} fusion(bf16[2048,1024]{1,0:T(8,128)(2,1)} %param.22, bf16[256,2048]{1,0:T(8,128)(2,1)S(1)} %copy-done.2, f32[2048]{0:T(1024)S(1)} %copy-done.5, f32[256]{0:T(256)S(1)} %add_rsqrt_fusion.5), kind=kOutput, calls=%fused_computation.134 | convolution fusion | flops 1075838976 | bytes 6300672 | tf_op jit(solution)/shard_map/dot_general | solution.py:89
  19.8 2.5 fusion.47
  24.9 1.9 pad_maximum_fusion
  26.8 8.6 %all-to-all-start = ((bf16[256,8,768]{2,0,1:T(8,128)(2,1)}), bf16[256,8,768]{2,0,1:T(8,128)(2,1)S(1)}, u32[]{:S(2)}, u32[]{:S(2)}) async-start(bf16[256,8,768]{2,0,1:T(8,128)(2,1)} %pad_maximum_fusion), calls=%async_computation | async-start | bytes 6291456 | tf_op jit(solution)/shard_map/all_to_all | solution.py:98
  40.4 6.2 %gather_fusion.2 = bf16[32,64,1024]{2,1,0:T(8,128)(2,1)} fusion(bf16[64,64,1024]{2,1,0:T(8,128)(2,1)} %param.30, s32[1024]{0:T(1024)S(1)} %pad_clamp_fusion.3), kind=kCustom, calls=%fused_computation.4 | custom fusion | bytes 8388736 | tf_op jit(solution)/shard_map/jit(_take)/gather | solution.py:120
  46.6 2.6 %broadcast_select_fusion.1 = bf16[32,64,1024]{2,1,0:T(8,128)(2,1)S(1)} fusion(bf16[32,64,1024]{2,1,0:T(8,128)(2,1)} %gather_fusion.2, pred[32]{0:T(512)(128)(4,1)S(1)} %compare_and_fusion.1), kind=kLoop, calls=%fused_computation.54 | loop fusion | flops 2097152 | bytes 8388640 | tf_op jit(solution)/shard_map/jit(_take)/select_n | solution.py:120
  49.3 2.4 slice_bitcast_fusion
  53.0 101.3 %collective-permute-done = bf16[1,16,64,1024]{3,2,1,0:T(8,128)(2,1)} collective-permute-done((bf16[1,16,64,1024]{3,2,1,0:T(8,128)(2,1)}, bf16[1,16,64,1024]{3,2,1,0:T(8,128)(2,1)}, u32[]{:S(2)}, u32[]{:S(2)}) %collective-permute-start) | collective-permute-done | bytes 2097184 | tf_op jit(solution)/shard_map/ppermute | solution.py:26
  155.1 3.2 %fusion.34 = bf16[2,16,64,512]{3,2,1,0:T(8,128)(2,1)} fusion(s32[]{:T(128)} %select_n.267, bf16[1,16,64,1024]{3,2,1,0:T(8,128)(2,1)} %collective-permute-done, bf16[1,16,64,1024]{3,2,1,0:T(8,128)(2,1)} %collective-permute-done.1), kind=kLoop, calls=%fused_computation.65 | loop fusion | flops 4194304 | bytes 6291460 | tf_op jit(solution)/shard_map/stack | solution.py:124
  160.1 63.5 %while.15 = (s32[]{:T(128)}, bf16[4,512,256]{2,1,0:T(8,128)(2,1)}, s32[4]{0:T(128)S(1)}, s32[]{:T(128)}, s32[64]{0:T(128)S(1)}, /*index=5*/s32[]{:T(128)}, s32[6...) while((s32[]{:T(128)}, bf16[4,512,256]{2,1,0:T(8,128)(2,1)}, ...), condition=%wide.region_12.14_spmd, body=%wide.region_7.13_spmd.sunk | while | flops 816841920 | bytes 28617216 | solution.py:175
  162.4 4.1 %gather_fusion = bf16[16,64,1024]{2,1,0:T(8,128)(2,1)S(1)} fusion(bf16[64,64,1024]{2,1,0:T(8,128)(2,1)} %get-tuple-element.512, s32[1024]{0:T(1024)S(1)} %pad_clamp_fusion.6), kind=kCustom, calls=%fused_computation.1.clone.1 | custom fusion | bytes 4194368 | tf_op jit(solution)/shard_map/while/body/eval_jaxpr/jit(_take)/gather | solution.py:134
  167.0 1.8 bitcast_select_fusion.3
  178.3 4.1 %gather_fusion = bf16[16,64,1024]{2,1,0:T(8,128)(2,1)S(1)} fusion(bf16[64,64,1024]{2,1,0:T(8,128)(2,1)} %get-tuple-element.512, s32[1024]{0:T(1024)S(1)} %pad_clamp_fusion.6), kind=kCustom, calls=%fused_computation.1.clone.1 | custom fusion | bytes 4194368 | tf_op jit(solution)/shard_map/while/body/eval_jaxpr/jit(_take)/gather | solution.py:134
  182.9 1.8 bitcast_select_fusion.3
  194.2 4.1 %gather_fusion = bf16[16,64,1024]{2,1,0:T(8,128)(2,1)S(1)} fusion(bf16[64,64,1024]{2,1,0:T(8,128)(2,1)} %get-tuple-element.512, s32[1024]{0:T(1024)S(1)} %pad_clamp_fusion.6), kind=kCustom, calls=%fused_computation.1.clone.1 | custom fusion | bytes 4194368 | tf_op jit(solution)/shard_map/while/body/eval_jaxpr/jit(_take)/gather | solution.py:134
  210.1 4.1 %gather_fusion = bf16[16,64,1024]{2,1,0:T(8,128)(2,1)S(1)} fusion(bf16[64,64,1024]{2,1,0:T(8,128)(2,1)} %get-tuple-element.512, s32[1024]{0:T(1024)S(1)} %pad_clamp_fusion.6), kind=kCustom, calls=%fused_computation.1.clone.1 | custom fusion | bytes 4194368 | tf_op jit(solution)/shard_map/while/body/eval_jaxpr/jit(_take)/gather | solution.py:134
  223.6 7.3 %all-to-all-start.1 = ((bf16[8,256,256]{2,1,0:T(8,128)(2,1)}), bf16[8,256,256]{2,1,0:T(8,128)(2,1)}, u32[]{:S(2)}, u32[]{:S(2)}) async-start(bf16[8,256,256]{2,1,0:T(8,128)(2,1)} %bitcast.144), calls=%async_computation.1 | async-start | bytes 2097152 | tf_op jit(solution)/shard_map/all_to_all | solution.py:178
  230.9 2.5 multiply_reduce_fusion
  233.4 9.4 %all-to-all-done.1 = bf16[8,256,256]{2,1,0:T(8,128)(2,1)} async-done(((bf16[8,256,256]{2,1,0:T(8,128)(2,1)}), bf16[8,256,256]{2,1,0:T(8,128)(2,1)}, u32[]{:S(2)}, u32[]{:S(2)}) %all-to-all-start.1) | async-done | bytes 1048608 | tf_op jit(solution)/shard_map/all_to_all | solution.py:178
  242.8 2.3 copy.63
  245.1 6.2 %multiply_reduce_fusion.1 = (f32[256]{0:T(256)S(1)}, f32[256,2048]{1,0:T(8,128)S(1)}) fusion(bf16[256,2048]{0,1:T(8,128)(2,1)} %bitcast.142, bf16[2048,2048]{1,0:T(8,128)(2,1)} %all-gather.2.cloned.1.call-done), kind=kOutput, calls=%fused_computation.69 | convolution fusion | flops 2148531968 | bytes 11535360 | tf_op jit(solution)/shard_map/dot_general | solution.py:186
  251.3 2.0 fusion.33
  (160 shorter events, 51.0 us)
Async XLA Ops:
  6.5 224.3 %copy-start = (bf16[64,2048]{1,0:T(8,128)(2,1)S(1)}, bf16[64,2048]{1,0:T(8,128)(2,1)}, u32[]{:S(2)}) copy-start(bf16[64,2048]{1,0:T(8,128)(2,1)} %param.27) | copy-start | bytes 786436
  6.5 4.8 %copy-start.2 = (bf16[256,2048]{1,0:T(8,128)(2,1)S(1)}, bf16[256,2048]{1,0:T(8,128)(2,1)}, u32[]{:S(2)}) copy-start(bf16[256,2048]{1,0:T(8,128)(2,1)} %param.19) | copy-start | bytes 3145732
  6.5 5.1 %copy-start.5 = (f32[2048]{0:T(1024)S(1)}, f32[2048]{0:T(1024)}, u32[]{:S(2)}) copy-start(f32[2048]{0:T(1024)} %param.20) | copy-start | bytes 24580
  16.0 2.2 copy-start.9
  16.0 3.8 %copy-start.12 = (bf16[2048,2048]{1,0:T(8,128)(2,1)S(1)}, bf16[2048,2048]{1,0:T(8,128)(2,1)}, u32[]{:S(2)}) copy-start(bf16[2048,2048]{1,0:T(8,128)(2,1)} %param.21) | copy-start | bytes 25165828
  23.2 0.7 copy-start.10
  26.8 9.4 %copy-start.11 = (s32[64]{0:T(128)S(1)}, s32[64]{0:T(128)}, u32[]{:S(2)}) copy-start(s32[64]{0:T(128)} %param.33) | copy-start | bytes 772
  26.8 11.4 %copy-start.8 = (s32[64,16]{0,1:T(8,128)S(1)}, s32[64,16]{0,1:T(8,128)}, u32[]{:S(2)}) copy-start(s32[64,16]{0,1:T(8,128)} %param.31) | copy-start | bytes 12292
  26.8 131.4 %all-to-all-start = ((bf16[256,8,768]{2,0,1:T(8,128)(2,1)}), bf16[256,8,768]{2,0,1:T(8,128)(2,1)S(1)}, u32[]{:S(2)}, u32[]{:S(2)}) async-start(bf16[256,8,768]{2,0,1:T(8,128)(2,1)} %pad_maximum_fusion), calls=%async_computation | async-start | bytes 6291456 | tf_op jit(solution)/shard_map/all_to_all | solution.py:98
  35.5 209.6 %all-gather.2.cloned.1.call-start = ((), (), s32[]{:S(2)}) async-start(), calls=%async_computation.2 | async-start | bytes 8912896 | tf_op jit(solution)/shard_map/all_gather | solution.py:188
  51.7 102.6 %collective-permute-start = (bf16[1,16,64,1024]{3,2,1,0:T(8,128)(2,1)}, bf16[1,16,64,1024]{3,2,1,0:T(8,128)(2,1)}, u32[]{:S(2)}, u32[]{:S(2)}) collective-permute-start(bf16[1,16,64,1024]{3,2,1,0:T(8,128)(2,1)} %get-tuple-element.336), channel_id=1, source_target_pairs={{0,8},{8,16},{16,24},{24,32},{32,40},{40,48},{48,56},{56,64},{64,7... | collective-permute-start | bytes 6291464 | tf_op jit(solution)/shard_map/ppermute | solution.py:26
  53.0 102.2 %collective-permute-start.1 = (bf16[1,16,64,1024]{3,2,1,0:T(8,128)(2,1)}, bf16[1,16,64,1024]{3,2,1,0:T(8,128)(2,1)}, u32[]{:S(2)}, u32[]{:S(2)}) collective-permute-start(bf16[1,16,64,1024]{3,2,1,0:T(8,128)(2,1)} %get-tuple-element.335), channel_id=1, source_target_pairs={{8,0},{16,8},{24,16},{32,24},{40,32},{48,40},{56,48},{64,56},{72,6... | collective-permute-start | bytes 6291464 | tf_op jit(solution)/shard_map/ppermute | solution.py:29
  158.3 1.8 copy-start.1
  167.0 3.6 %copy-start.4 = (bf16[2048,1,256]{2,0,1:T(8,128)(2,1)S(1)}, bf16[2048,1,256]{2,0,1:T(8,128)(2,1)}, u32[]{:S(2)}) copy-start(bf16[2048,1,256]{2,0,1:T(8,128)(2,1)} %get-tuple-element.517) | copy-start | bytes 3145732 | tf_op jit(solution)/shard_map/while
  182.9 3.6 %copy-start.4 = (bf16[2048,1,256]{2,0,1:T(8,128)(2,1)S(1)}, bf16[2048,1,256]{2,0,1:T(8,128)(2,1)}, u32[]{:S(2)}) copy-start(bf16[2048,1,256]{2,0,1:T(8,128)(2,1)} %get-tuple-element.517) | copy-start | bytes 3145732 | tf_op jit(solution)/shard_map/while
  198.8 3.6 %copy-start.4 = (bf16[2048,1,256]{2,0,1:T(8,128)(2,1)S(1)}, bf16[2048,1,256]{2,0,1:T(8,128)(2,1)}, u32[]{:S(2)}) copy-start(bf16[2048,1,256]{2,0,1:T(8,128)(2,1)} %get-tuple-element.517) | copy-start | bytes 3145732 | tf_op jit(solution)/shard_map/while
  214.6 3.6 %copy-start.4 = (bf16[2048,1,256]{2,0,1:T(8,128)(2,1)S(1)}, bf16[2048,1,256]{2,0,1:T(8,128)(2,1)}, u32[]{:S(2)}) copy-start(bf16[2048,1,256]{2,0,1:T(8,128)(2,1)} %get-tuple-element.517) | copy-start | bytes 3145732 | tf_op jit(solution)/shard_map/while
  223.6 7.3 %copy-start.3 = (bf16[256,2048]{1,0:T(8,128)(2,1)S(1)}, bf16[256,2048]{1,0:T(8,128)(2,1)}, u32[]{:S(2)}) copy-start(bf16[256,2048]{1,0:T(8,128)(2,1)} %param.19) | copy-start | bytes 3145732
  223.6 19.2 %all-to-all-start.1 = ((bf16[8,256,256]{2,1,0:T(8,128)(2,1)}), bf16[8,256,256]{2,1,0:T(8,128)(2,1)}, u32[]{:S(2)}, u32[]{:S(2)}) async-start(bf16[8,256,256]{2,1,0:T(8,128)(2,1)} %bitcast.144), calls=%async_computation.1 | async-start | bytes 2097152 | tf_op jit(solution)/shard_map/all_to_all | solution.py:178
  245.1 6.2 %copy-start.6 = (f32[2048]{0:T(1024)S(1)}, f32[2048]{0:T(1024)}, u32[]{:S(2)}) copy-start(f32[2048]{0:T(1024)} %param.28) | copy-start | bytes 24580
  245.1 6.2 %copy-start.7 = (f32[2048]{0:T(1024)S(1)}, f32[2048]{0:T(1024)}, u32[]{:S(2)}) copy-start(f32[2048]{0:T(1024)} %param.29) | copy-start | bytes 24580
Sparse Core Ops, SparseCore 0:
  38.0 105.9 all-gather.1
where the time goes:
time: 261 us; the launch traced here: 260 us
  waiting for transfers between devices  112 us (43%)
  local copies, waits for them, and re-layouts  47.2 us (18%)
  matrix products  30.1 us (12%)
  other arithmetic  29.9 us (11%)
  starting transfers between devices  17.4 us (7%)
  between operations  13.8 us (5%)
  loops' own time  9.8 us (4%)
    ppermute x1, waiting for transfers between devices, extended_2(): lax.ppermute(lax.slice_in_dim(block, block.shape[dim] - width, None, axis...  101 us
    gather x4, local copies, waits for them, and re-layouts, one_slot(): jnp.take(cache_pool, local_pages, axis=0)  16.3 us
    another operation x1, loops' own time, shards(): lax.map(one_slot, jnp.arange(REQ_DEV, dtype=jnp.int32))  9.8 us
    all_to_all x1, waiting for transfers between devices, shards(): lax.all_to_all(attended.reshape(head_count, tok_rows, query_width), 'head...  9.42 us
    all_to_all x1, starting transfers between devices, shards(): lax.all_to_all(outgoing, 'head', split_axis=1, concat_axis=0, tiled=True)  8.62 us
    select_n x4, other arithmetic, one_slot(): jnp.where(home_group == group, stayed, jnp.where(home_group == before, ar...  7.35 us
    all_to_all x1, starting transfers between devices, shards(): lax.all_to_all(attended.reshape(head_count, tok_rows, query_width), 'head...  7.29 us
    gather x1, local copies, waits for them, and re-layouts, shards(): jnp.take(cache_pool, mover_pages.reshape(-1), axis=0)  6.17 us
  transfers between devices with their start and end apart: 5, of which 3 were waited for; matrix products, arithmetic and copies ran while one was open for 30% of the time, Pallas kernels for 0%

commit v1 on v0

v1 whole, which is shorter than its diff:
```python
import functools
import math

import jax
import jax.numpy as jnp
from jax import lax
from jax.experimental import pallas as pl
from jax.experimental.pallas import tpu as pltpu
from jax.sharding import PartitionSpec as P

MESH = pl.DeviceIdType.MESH
F32 = jnp.float32
BF16 = jnp.bfloat16

D = 2048
NH = 8
KVH = 2
HD = 256
HALF = HD // 2
RANK = 64
REQ_DEV = 4
CH = 512
LMAX = 1024
PAGE = 64
MAXP = 16
GROUPS = 16
NREQ = 64
ROWS = 256
KVW = 2 * KVH * HD
WROWS = D // GROUPS
UNIT = WROWS // 4
QPAGES = MAXP // 4
HPAGES = QPAGES // 2
EPS = 1e-06
VMEM_LIMIT = 64 * 1024 * 1024 - 128 * 1024


def place():
    group = lax.axis_index("req")
    member = lax.axis_index("head")
    x = group // 4
    y_lo = (group // 2) % 2
    core = group % 2
    z = member // 2
    y_hi = member % 2
    return group, x, y_lo, core, z, y_hi


def gather_kernel(table, slots, pool, own, chip, cross, sems):
    group, _, _, core, z, y_hi = place()
    slot = group * REQ_DEV + z
    request = lax.fori_loop(
        0, NREQ, lambda i, found: jnp.where(slots[i] == slot, i, found), jnp.int32(0)
    )
    partner = group + 1 - 2 * core
    across = (group + 2 * core - 1 + GROUPS) % GROUPS
    base = group * REQ_DEV
    to_chip = base
    to_cross = base
    for i in range(REQ_DEV):
        aim = slots[base + i] // REQ_DEV
        to_chip = jnp.where(aim == partner, base + i, to_chip)
        to_cross = jnp.where(aim == across, base + i, to_cross)
    copies = []
    first = z * QPAGES + y_hi * HPAGES
    for p in range(HPAGES):
        copies.append((table[to_cross * MAXP + first + p], cross.at[pl.ds(p * PAGE, PAGE)]))
    for p in range(MAXP):
        copies.append((table[to_chip * MAXP + p], chip.at[pl.ds(p * PAGE, PAGE)]))
    for p in range(MAXP):
        copies.append((table[request * MAXP + p], own.at[pl.ds(p * PAGE, PAGE)]))
    started = [
        pltpu.make_async_copy(pool.at[page], target, sems.at[i])
        for i, (page, target) in enumerate(copies)
    ]
    for copy in started:
        copy.start()
    for copy in started:
        copy.wait()


def gather_pages(page_table, slot_of, cache_pool):
    smem = pl.BlockSpec(memory_space=pltpu.SMEM)
    vmem = pl.BlockSpec(memory_space=pltpu.VMEM)
    return pl.pallas_call(
        gather_kernel,
        out_shape=(
            jax.ShapeDtypeStruct((LMAX, KVW), BF16),
            jax.ShapeDtypeStruct((LMAX, KVW), BF16),
            jax.ShapeDtypeStruct((HPAGES * PAGE, KVW), BF16),
        ),
        in_specs=[smem, smem, pl.BlockSpec(memory_space=pl.ANY)],
        out_specs=(vmem, vmem, vmem),
        scratch_shapes=[pltpu.SemaphoreType.DMA((2 * MAXP + HPAGES,))],
        name="gather_pages",
    )(page_table.reshape(-1), slot_of, cache_pool)


N_COPIES = 64
CROSS_ID = 1


def params(**kw):
    return pltpu.CompilerParams(vmem_limit_bytes=VMEM_LIMIT, **kw)


def comm_kernel(w_ref, chip_ref, cross_ref, full, chip_in, cross_in, ssem, rsem, lsem):
    group, x, yl, c, z, h = place()

    def dev(ax, ayl, ac, az, ah):
        return (ax * 4 + ayl * 2 + ac, az * 2 + ah)

    xp, xm, x2 = (x + 1) % 4, (x + 3) % 4, (x + 2) % 4
    zp, zm, z2 = (z + 1) % 4, (z + 3) % 4, (z + 2) % 4
    ol = 1 - yl
    to_xp, to_xm = dev(xp, yl, c, z, h), dev(xm, yl, c, z, h)
    to_zp, to_zm = dev(x, yl, c, zp, h), dev(x, yl, c, zm, h)
    to_s, to_c = dev(x, ol, c, z, h), dev(x, ol, c, z, 1 - h)
    to_p = dev(x, yl, 1 - c, z, h)
    across = (group + 2 * c - 1 + GROUPS) % GROUPS
    to_t = [(across, z * 2 + h), (across, z * 2 + 1 - h)]

    barrier = pltpu.get_barrier_semaphore()
    others = [to_xp, to_xm, to_zp, to_zm, to_s, to_c, to_p] + to_t
    for other in others:
        pl.semaphore_signal(barrier, inc=1, device_id=other, device_id_type=MESH)
    pl.semaphore_wait(barrier, len(others))

    sent = []

    def send(src, dst, to):
        i = len(sent)
        copy = pltpu.make_async_remote_copy(
            src_ref=src,
            dst_ref=dst,
            send_sem=ssem.at[i],
            recv_sem=rsem.at[i],
            device_id=to,
            device_id_type=MESH,
        )
        copy.start()
        sent.append(copy)
        return copy

    def rows(ax, ayl, unit, n):
        start = (ax * 4 + ayl * 2 + c) * WROWS + unit * UNIT
        return full.at[pl.ds(pl.multiple_of(start, UNIT), n * UNIT)]

    def mine(unit, n):
        return w_ref.at[pl.ds(unit * UNIT, n * UNIT)]

    def pages(az, rel, p, n):
        half = h if rel == 0 else 1 - h
        start = (az * QPAGES + half * HPAGES + p) * PAGE
        return cross_in.at[pl.ds(pl.multiple_of(start, PAGE), n * PAGE)]

    def relay(ref, to):
        return send(ref, ref, to)

    own_copy = pltpu.make_async_copy(w_ref, rows(x, yl, 0, 4), lsem)
    own_copy.start()
    crossing = []
    for p in range(HPAGES):
        for rel in range(2):
            target = (z * QPAGES + h * HPAGES + p) * PAGE
            crossing.append(
                send(
                    cross_ref.at[pl.ds(p * PAGE, PAGE)],
                    cross_in.at[pl.ds(pl.multiple_of(target, PAGE), PAGE)],
                    to_t[rel],
                )
            )
    a1 = [send(mine(0, 2), rows(x, yl, 0, 2), to) for to in (to_xp, to_xm)]
    b1 = [send(mine(2, 1), rows(x, yl, 2, 1), to_s), send(mine(3, 1), rows(x, yl, 3, 1), to_c)]
    chip_copy = send(chip_ref, chip_in, to_p)
    last = [send(w_ref, rows(x, yl, 0, 4), to_p), chip_copy]
    b2 = [send(mine(2, 2), rows(x, yl, 2, 2), to) for to in (to_xp, to_xm)]
    last += [send(mine(0, 1), rows(x, yl, 0, 1), to_s), send(mine(1, 1), rows(x, yl, 1, 1), to_c)]

    ring = []
    for p in range(HPAGES):
        for rel in range(2):
            crossing[2 * p + rel].wait_recv()
            for to in (to_zp, to_zm):
                ring.append(relay(pages(z, rel, p, 1), to))
    for copy in b1:
        copy.wait_recv()
    b2y = [relay(rows(x, ol, 2, 2), to) for to in (to_xp, to_xm)]
    last.append(relay(rows(x, ol, 2, 2), to_p))
    for copy in a1:
        copy.wait_recv()
    a2 = [relay(rows(xm, yl, 0, 1), to_xp), relay(rows(xp, yl, 1, 1), to_xm)]
    for ax in (xm, xp):
        last += [relay(rows(ax, yl, 0, 1), to_s), relay(rows(ax, yl, 1, 1), to_c)]
        last.append(relay(rows(ax, yl, 0, 2), to_p))
    for copy in b2:
        copy.wait_recv()
    b3 = [relay(rows(xm, yl, 2, 1), to_xp), relay(rows(xp, yl, 3, 1), to_xm)]
    for ax in (xm, xp):
        last.append(relay(rows(ax, yl, 2, 2), to_p))
    for p in range(HPAGES):
        for rel in range(2):
            one, two = ring[4 * p + 2 * rel], ring[4 * p + 2 * rel + 1]
            one.wait_recv()
            two.wait_recv()
            last.append(relay(pages(zm, 0, p, 1), to_zp) if rel == 0 else relay(pages(zp, 1, p, 1), to_zm))
    for copy in a2:
        copy.wait_recv()
    last += [relay(rows(x2, yl, 0, 1), to_s), relay(rows(x2, yl, 1, 1), to_c)]
    last.append(relay(rows(x2, yl, 0, 2), to_p))
    for copy in b2y:
        copy.wait_recv()
    b3 += [relay(rows(xm, ol, 2, 1), to_xp), relay(rows(xp, ol, 3, 1), to_xm)]
    for ax in (xm, xp):
        last.append(relay(rows(ax, ol, 2, 2), to_p))
    for copy in b3:
        copy.wait_recv()
    last.append(relay(rows(x2, yl, 2, 2), to_p))
    last.append(relay(rows(x2, ol, 2, 2), to_p))
    yin = [last[i] for i in (2, 3, 5, 6, 8, 9)]
    yin += [last[i] for i in (17, 18)]
    for i, ax in enumerate((x, xm, xp, x2)):
        yin[2 * i].wait_recv()
        yin[2 * i + 1].wait_recv()
        last.append(relay(rows(ax, ol, 0, 2), to_p))
    own_copy.wait()
    for copy in last:
        if not any(copy is done for done in yin):
            copy.wait_recv()
    for copy in sent:
        copy.wait_send()


def exchange(w_output, chip, cross):
    vmem = pl.BlockSpec(memory_space=pltpu.VMEM)
    return pl.pallas_call(
        comm_kernel,
        out_shape=(
            jax.ShapeDtypeStruct((D, D), BF16),
            jax.ShapeDtypeStruct((LMAX, KVW), BF16),
            jax.ShapeDtypeStruct((LMAX, KVW), BF16),
        ),
        in_specs=[vmem, vmem, vmem],
        out_specs=(vmem, vmem, vmem),
        scratch_shapes=[
            pltpu.SemaphoreType.DMA((N_COPIES,)),
            pltpu.SemaphoreType.DMA((N_COPIES,)),
            pltpu.SemaphoreType.DMA,
        ],
        compiler_params=params(collective_id=0, has_side_effects=True),
        name="exchange",
    )(w_output, chip, cross)


def rms(values):
    return lax.rsqrt(jnp.mean(values * values, axis=-1, keepdims=True) + EPS)


def dot(a, b):
    return jnp.dot(a, b, preferred_element_type=F32)


def rotated(values, cosine, sine):
    a, b = values[:, :HALF], values[:, HALF:]
    return jnp.concatenate([a * cosine - b * sine, b * cosine + a * sine], axis=-1)


def project_kernel(
    tokens, in_gain, wq, wkv, q_gain, k_gain, left, right, l_gain, cosine, sine,
    query, kv, side, normed,
):
    inputs = tokens[...].astype(F32)
    normed[...] = (inputs * rms(inputs) * in_gain[...]).astype(BF16)
    cos, sin = cosine[...], sine[...]
    for g in range(KVH):
        raw = dot(normed[...], wkv[:, 2 * g * HD : (2 * g + 2) * HD])
        key, value = raw[:, :HD], raw[:, HD:]
        key = rotated(key * rms(key) * k_gain[...], cos, sin)
        kv[:, 2 * g * HD : (2 * g + 1) * HD] = key.astype(BF16)
        kv[:, (2 * g + 1) * HD : (2 * g + 2) * HD] = (value * rms(value)).astype(BF16)

    def head(n, carry):
        raw = dot(normed[...], wq[:, pl.ds(pl.multiple_of(n * HD, HD), HD)])
        raw = rotated(raw * rms(raw) * q_gain[...], cosine[...], sine[...])
        query[n] = raw.astype(BF16)
        return carry

    lax.fori_loop(0, NH, head, 0)
    low = dot(normed[...], left[...]).astype(BF16)
    u = dot(low, right[...])
    laurel = normed[...].astype(F32) + u * rms(u) * l_gain[...]
    side[...] = tokens[...].astype(F32) + laurel


def attend_kernel(
    lens, slots, query, kv, other, own, chip_in, cross_in, full, side, p_gain,
    mixed, store, attended, projected, sems,
):
    group, _, _, core, z, y_hi = place()
    slot = group * REQ_DEV + z
    request = lax.fori_loop(
        0, NREQ, lambda i, found: jnp.where(slots[i] == slot, i, found), jnp.int32(0)
    )
    length = lens[request]
    home = request // REQ_DEV
    partner = group + 1 - 2 * core
    for want, source in (
        (home == group, own),
        (home == partner, chip_in),
        ((home != group) & (home != partner), cross_in),
    ):

        @pl.when(want)
        def _():
            copy = pltpu.make_async_copy(source, store, sems.at[0])
            copy.start()
            copy.wait()

    def contract(a, b):
        return lax.dot_general(a, b, (((1,), (1,)), ((), ())), preferred_element_type=F32)

    seen = lax.broadcasted_iota(jnp.int32, (1, LMAX), 1) < length
    causal = lax.broadcasted_iota(jnp.int32, (ROWS, ROWS), 1) <= lax.broadcasted_iota(
        jnp.int32, (ROWS, ROWS), 0
    )
    for g in range(KVH):
        k0, v0, end = 2 * g * HD, (2 * g + 1) * HD, (2 * g + 2) * HD

        def head(i, carry):
            n = g * (NH // KVH) + i
            q = query[n]
            cached = jnp.where(seen, contract(q, store[:, k0:v0]) * HD**-0.5, -jnp.inf)
            fresh = jnp.where(causal, contract(q, kv[:, k0:v0]) * HD**-0.5, -jnp.inf)
            past = contract(q, other[:, k0:v0]) * HD**-0.5
            past = jnp.where(y_hi == 1, past, -jnp.inf)
            top = jnp.maximum(
                jnp.maximum(jnp.max(cached, axis=-1, keepdims=True), jnp.max(past, axis=-1, keepdims=True)),
                jnp.max(fresh, axis=-1, keepdims=True),
            )
            cached, fresh, past = jnp.exp(cached - top), jnp.exp(fresh - top), jnp.exp(past - top)
            total = (
                jnp.sum(cached, axis=-1, keepdims=True)
                + jnp.sum(fresh, axis=-1, keepdims=True)
                + jnp.sum(past, axis=-1, keepdims=True)
            )
            scale = 1.0 / total
            result = dot((cached * scale).astype(BF16), store[:, v0:end])
            result += dot((fresh * scale).astype(BF16), kv[:, v0:end])
            result += dot((past * scale).astype(BF16), other[:, v0:end])
            attended[:, pl.ds(pl.multiple_of(n * HD, HD), HD)] = result.astype(BF16)
            return carry

        lax.fori_loop(0, NH // KVH, head, 0)

    def column(i, square):
        part = dot(attended[...], full[:, pl.ds(pl.multiple_of(i * HD, HD), HD)])
        projected[:, pl.ds(pl.multiple_of(i * HD, HD), HD)] = part
        return square + jnp.sum(part * part, axis=-1, keepdims=True)

    square = lax.fori_loop(0, D // HD, column, jnp.zeros((ROWS, 1), F32))
    scale = lax.rsqrt(square / D + EPS)
    attn = projected[...] * scale * p_gain[...]
    mixed[...] = ((attn + side[...]) / math.sqrt(2.0)).astype(BF16)


def vmem_call(kernel, out_shape, scratch, n_smem, name, args):
    smem = pl.BlockSpec(memory_space=pltpu.SMEM)
    vmem = pl.BlockSpec(memory_space=pltpu.VMEM)
    return pl.pallas_call(
        kernel,
        out_shape=out_shape,
        in_specs=[smem] * n_smem + [vmem] * (len(args) - n_smem),
        out_specs=jax.tree.map(lambda _: vmem, out_shape),
        scratch_shapes=scratch,
        compiler_params=params(),
        name=name,
    )(*args)


def shards(
    tokens, input_gain, w_query, w_keyval, query_gain, key_gain, w_output, laurel_left,
    laurel_right, laurel_gain, post_gain, cache_pool, page_table, cached_len, slot_of,
):
    group, _, _, _, z, y_hi = place()
    own, chip, cross = gather_pages(page_table, slot_of, cache_pool)
    full, chip_in, cross_in = exchange(w_output, chip, cross)
    slot = group * REQ_DEV + z
    start = jnp.sum(jnp.where(slot_of == slot, cached_len, 0))
    position = start + y_hi * ROWS + jnp.arange(ROWS, dtype=jnp.int32)
    inverse = jnp.power(jnp.float32(1000000.0), -jnp.arange(HALF, dtype=F32) * (2.0 / HD))
    angle = position.astype(F32)[:, None] * inverse[None, :]
    query, kv, side = vmem_call(
        project_kernel,
        (
            jax.ShapeDtypeStruct((NH, ROWS, HD), BF16),
            jax.ShapeDtypeStruct((ROWS, KVW), BF16),
            jax.ShapeDtypeStruct((ROWS, D), F32),
        ),
        [pltpu.VMEM((ROWS, D), BF16)],
        0,
        "project",
        (
            tokens, input_gain[None], w_query, w_keyval, query_gain[None], key_gain[None],
            laurel_left, laurel_right, laurel_gain[None], jnp.cos(angle), jnp.sin(angle),
        ),
    )
    other = lax.ppermute(kv, "head", [(2 * i, 2 * i + 1) for i in range(4)])
    return vmem_call(
        attend_kernel,
        jax.ShapeDtypeStruct((ROWS, D), BF16),
        [
            pltpu.VMEM((LMAX, KVW), BF16),
            pltpu.VMEM((ROWS, D), BF16),
            pltpu.VMEM((ROWS, D), F32),
            pltpu.SemaphoreType.DMA((1,)),
        ],
        2,
        "attend",
        (
            cached_len, slot_of, query, kv, other, own, chip_in, cross_in, full, side,
            post_gain[None],
        ),
    )


def solution(mesh):
    in_specs = (
        P(("req", "head"), None),
        P(), P(), P(), P(), P(),
        P("req", None),
        P(), P(), P(), P(),
        P("req", None, None),
        P(), P(), P(),
    )
    out_specs = P(("req", "head"), None)
    return jax.shard_map(shards, mesh=mesh, in_specs=in_specs, out_specs=out_specs, check_vma=False)
```

time: 261 us -> 107 us (0.41)
  waiting for transfers between devices: 112 us -> 0.01 us
  Pallas kernels: 0 us -> 93.9 us
  local copies, waits for them, and re-layouts: 47.2 us -> 2.71 us
  matrix products: 30.1 us -> 0 us
  other arithmetic: 29.9 us -> 2.55 us
  between operations: 13.8 us -> 0.72 us
  starting transfers between devices: 17.4 us -> 6.42 us
  loops' own time: 9.8 us -> 0 us
    ppermute x2 -> x1, waiting for transfers between devices: 102 us -> 0.01 us  [shards(): other = lax.ppermute(kv, 'head', [(2 * i, 2 * i + 1) for i in range(4)])]
    pallas_call x0 -> x4, Pallas kernels: none -> 93.9 us  [the longest x1 49.9 us: exchange(): pl.pallas_call(comm_kernel, out_shape=(jax.ShapeDtypeStruct((D, D), BF16)...]
    dot_general x20 -> x0, matrix products: 30.1 us -> none  [the longest x1 6.16 us: shards(): jnp.dot(returned, lax.all_gather(w_output, 'req', axis=0, tiled=True), pr...]
    gather x8 -> x0, local copies, waits for them, and re-layouts: 26.8 us -> none  [the longest x4 16.3 us: one_slot(): jnp.take(cache_pool, local_pages, axis=0)]
    all_to_all x2 -> x0, starting transfers between devices: 15.9 us -> none  [the longest x1 8.62 us: shards(): lax.all_to_all(outgoing, 'head', split_axis=1, concat_axis=0, tiled=True)]
    select_n x18 -> x0, other arithmetic: 13.1 us -> none  [the longest x4 7.35 us: one_slot(): jnp.where(home_group == group, stayed, jnp.where(home_group == before, ar...]
    another operation x1 -> x0, loops' own time: 9.8 us -> none  [shards(): lax.map(one_slot, jnp.arange(REQ_DEV, dtype=jnp.int32))]
    all_to_all x2 -> x0, waiting for transfers between devices: 9.43 us -> none  [the longest x1 9.42 us: shards(): lax.all_to_all(attended.reshape(head_count, tok_rows, query_width), 'head...]
  transfers between devices with their start and end apart: 5 -> 1, of which waited for: 3 -> 0; matrix products, arithmetic and copies ran while one was open for 30% -> 1% of each run, Pallas kernels for 0% -> 53%
where the time goes in v1:
time: 107 us; the launch traced here: 106 us
  Pallas kernels  93.9 us (88%)
  starting transfers between devices  6.42 us (6%)
  local copies, waits for them, and re-layouts  2.71 us (3%)
  other arithmetic  2.55 us (2%)
    pallas_call x1, Pallas kernels, exchange(): pl.pallas_call(comm_kernel, out_shape=(jax.ShapeDtypeStruct((D, D), BF16)...  49.9 us
    pallas_call x2, Pallas kernels, vmem_call(): pl.pallas_call(kernel, out_shape=out_shape, in_specs=[smem] * n_smem + [v...  37.9 us
    ppermute x1, starting transfers between devices, shards(): other = lax.ppermute(kv, 'head', [(2 * i, 2 * i + 1) for i in range(4)])  6.42 us
    pallas_call x1, Pallas kernels, gather_pages(): pl.pallas_call(gather_kernel, out_shape=(jax.ShapeDtypeStruct((LMAX, KVW)...  6.14 us
  transfers between devices with their start and end apart: 1, of which 0 were waited for; matrix products, arithmetic and copies ran while one was open for 1% of the time, Pallas kernels for 53%

profile of v1, /device:TPU:1, one launch (start us, length us, event | category | flops | bytes accessed | tf_op | source)
XLA Modules:
  0.0 106.3 jit_solution(14325879215788759764)
XLA Ops:
  0.0 1.3 %fusion = s32[]{:T(128)} fusion(s32[64]{0:T(128)} %lens.1, s32[64]{0:T(128)} %slots.3, s32[]{:T(128)S(6)} %add.21), kind=kLoop, calls=%fused_computation.4 | loop fusion | flops 191 | bytes 520 | tf_op jit(solution)/shard_map/reduce_sum | solution.py:388
  2.0 2.0 %copy.17.left = bf16[2048,64]{1,0:T(8,128)(2,1)} copy(bf16[2048,64]{0,1:T(8,128)(2,1)} %param.22) | data formatting | bytes 524288 | tf_op args[7]
  4.0 1.2 %multiply_sine_fusion = (f32[256,128]{1,0:T(8,128)}, f32[256,128]{1,0:T(8,128)}) fusion(f32[128]{0:T(128)S(1)} %multiply_power_fusion, f32[256]{0:T(256)S(1)} %add_convert_fusion), kind=kLoop, calls=%fused_computation | loop fusion | flops 32768 | bytes 263680 | tf_op jit(solution)/shard_map/sin | solution.py:404
  5.2 0.0 copy-start
  5.2 13.9 %project.1 = (bf16[8,256,256]{2,1,0:T(8,128)(2,1)}, bf16[256,1024]{1,0:T(8,128)(2,1)}, f32[256,2048]{1,0:T(8,128)}) custom-call(bf16[256,2048]{1,0:T(8,128)(2,1)} %tokens.1, f32[1,2048]{1,0:T(1,128)} %bitcast.5, bf16[2048,2048]{1,0:T(8,128)(2,1)} %wq.1, bf16[2048,1024]{1,0:T(8,128)(2,1)} %wkv.1, f32[1,256]{1,0:T(1,128)} %bitcast.8, f32[1,256]{1,0:T(1,128)} %bitcast.9, ...), custom_call_target="tpu_custom_call" | custom-call | tf_op jit(solution)/shard_map/project/pallas_call | solution.py:369
  19.1 6.4 %collective-permute-start = (bf16[256,1024]{1,0:T(8,128)(2,1)}, bf16[256,1024]{1,0:T(8,128)(2,1)}, u32[]{:S(2)}, u32[]{:S(2)}) collective-permute-start(bf16[256,1024]{1,0:T(8,128)(2,1)} %get-tuple-element.15.kv), channel_id=1, source_target_pairs={{0,1},{2,3},{4,5},{6,7},{8,9},{10,11},{12,13},{14,15},{16,17},{18,... | collective-permute-start | bytes 1572872 | tf_op jit(solution)/shard_map/ppermute | solution.py:407
  25.5 0.0 copy-done
  25.5 0.1 copy.18
  25.6 0.7 reshape.14.table
  26.3 6.1 %gather_pages.1 = (bf16[1024,1024]{1,0:T(8,128)(2,1)}, bf16[1024,1024]{1,0:T(8,128)(2,1)}, bf16[128,1024]{1,0:T(8,128)(2,1)}) custom-call(s32[1024]{0:T(1024)} %reshape.14.table, s32[64]{0:T(128)} %slots.3, bf16[64,64,1024]{2,1,0:T(8,128)(2,1)} %pool.1), custom_call_target="tpu_custom_call" | custom-call | tf_op jit(solution)/shard_map/gather_pages/pallas_call | solution.py:85
  32.4 49.9 %exchange.1 = (bf16[2048,2048]{1,0:T(8,128)(2,1)}, bf16[1024,1024]{1,0:T(8,128)(2,1)}, bf16[1024,1024]{1,0:T(8,128)(2,1)}) custom-call(bf16[128,2048]{1,0:T(8,128)(2,1)} %w_ref.1, bf16[1024,1024]{1,0:T(8,128)(2,1)} %get-tuple-element.17.chip_ref, bf16[128,1024]{1,0:T(8,128)(2,1)} %get-tuple-element.18.cross_ref), custom_call_target="tpu_custom_call" | custom-call | tf_op jit(solution)/shard_map/exchange/pallas_call | solution.py:236
  82.3 0.0 collective-permute-done.other
  82.3 24.0 %attend.1 = bf16[256,2048]{1,0:T(8,128)(2,1)} custom-call(s32[64]{0:T(128)} %lens.1, s32[64]{0:T(128)} %slots.3, bf16[8,256,256]{2,1,0:T(8,128)(2,1)} %get-tuple-element.14.query, bf16[256,1024]{1,0:T(8,128)(2,1)} %get-tuple-element.15.kv, bf16[256,1024]{1,0:T(8,128)(2,1)} %collective-permute-done.other, bf16[1024,1024]{1,0:T(8,128)(2,1)} %get-tuple-element.16.own, ...), custom_call_target="tpu_custom_call" | custom-call | tf_op jit(solution)/shard_map/attend/pallas_call | solution.py:369
  (2 shorter events, 0.0 us)
Async XLA Ops:
  5.2 20.3 %copy-start = (s32[64,16]{0,1:T(8,128)S(1)}, s32[64,16]{0,1:T(8,128)}, u32[]{:S(2)}) copy-start(s32[64,16]{0,1:T(8,128)} %param.27) | copy-start | bytes 12292
  19.1 63.2 %collective-permute-start = (bf16[256,1024]{1,0:T(8,128)(2,1)}, bf16[256,1024]{1,0:T(8,128)(2,1)}, u32[]{:S(2)}, u32[]{:S(2)}) collective-permute-start(bf16[256,1024]{1,0:T(8,128)(2,1)} %get-tuple-element.15.kv), channel_id=1, source_target_pairs={{0,1},{2,3},{4,5},{6,7},{8,9},{10,11},{12,13},{14,15},{16,17},{18,... | collective-permute-start | bytes 1572872 | tf_op jit(solution)/shard_map/ppermute | solution.py:407

commit v2 on v0

v2 whole, which is shorter than its diff:
```python
import math

import jax
import jax.numpy as jnp
import numpy as np
from jax import lax
from jax.experimental import pallas as pl
from jax.experimental.pallas import tpu as pltpu
from jax.sharding import PartitionSpec as P

MESH = pl.DeviceIdType.MESH
F32 = jnp.float32
BF16 = jnp.bfloat16

D = 2048
NH = 8
KVH = 2
PER_KV = NH // KVH
HD = 256
HALF = HD // 2
RANK = 64
REQ_DEV = 4
CH = 512
LMAX = 1024
PAGE = 64
MAXP = 16
POOL = 64
GROUPS = 16
NREQ = 64
ROWS = 256
KVW = 2 * KVH * HD
WROWS = D // GROUPS
UNIT = WROWS // 4
QPAGES = MAXP // 4
HPAGES = QPAGES // 2
EPS = 1e-06
CROSS_AT = MAXP
N_COPIES = 72
VMEM_LIMIT = 64 * 1024 * 1024 - 128 * 1024
INVERSE = np.power(1000000.0, -np.arange(HALF) * (2.0 / HD)).astype(np.float32)[None]


def rms(values):
    return lax.rsqrt(jnp.mean(values * values, axis=-1, keepdims=True) + EPS)


def dot(a, b):
    return jnp.dot(a, b, preferred_element_type=F32)


def contract(a, b):
    return lax.dot_general(a, b, (((1,), (1,)), ((), ())), preferred_element_type=F32)


def rotated(values, cosine, sine):
    a, b = values[:, :HALF], values[:, HALF:]
    return jnp.concatenate([a * cosine - b * sine, b * cosine + a * sine], axis=-1)


def block_kernel(
    table, lens, slots,
    in_gain, q_gain, k_gain, left_t, right, l_gain, p_gain, inverse,
    tokens_hbm, wq_hbm, wkv_hbm, w_ref, pool,
    mixed,
    tokens, wq, wkv, full, store, moved, chip_out, cross_out, cache,
    normed, cosine, sine, query, kv, other, side, attended, projected, tops, totals, sums,
    ssem, rsem, lsem,
):
    group = lax.axis_index("req")
    member = lax.axis_index("head")
    x, yl, c = group // 4, (group // 2) % 2, group % 2
    z, h = member // 2, member % 2

    def dev(ax, ayl, ac, az, ah):
        return (ax * 4 + ayl * 2 + ac, az * 2 + ah)

    xp, xm, x2 = (x + 1) % 4, (x + 3) % 4, (x + 2) % 4
    zp, zm = (z + 1) % 4, (z + 3) % 4
    ol = 1 - yl
    to_xp, to_xm = dev(xp, yl, c, z, h), dev(xm, yl, c, z, h)
    to_zp, to_zm = dev(x, yl, c, zp, h), dev(x, yl, c, zm, h)
    to_s, to_c = dev(x, ol, c, z, h), dev(x, ol, c, z, 1 - h)
    to_p = dev(x, yl, 1 - c, z, h)
    to_o = dev(x, yl, c, z, 1 - h)
    partner = group + 1 - 2 * c
    across = (group + 2 * c - 1 + GROUPS) % GROUPS
    to_t = [(across, z * 2 + h), (across, z * 2 + 1 - h)]

    barrier = pltpu.get_barrier_semaphore()
    peers = [to_xp, to_xm, to_zp, to_zm, to_s, to_c, to_p, to_o] + to_t
    for peer in peers:
        pl.semaphore_signal(barrier, inc=1, device_id=peer, device_id_type=MESH)

    loads = []

    def load(src, dst):
        copy = pltpu.make_async_copy(src, dst, lsem.at[len(loads)])
        copy.start()
        loads.append(copy)
        return copy

    pool_in = load(pool, store)
    tokens_in = load(tokens_hbm, tokens)
    wkv_in = load(wkv_hbm, wkv)
    wq_in = [load(wq_hbm.at[:, pl.ds(i * 2 * HD, 2 * HD)], wq.at[:, pl.ds(i * 2 * HD, 2 * HD)]) for i in range(4)]

    def rows(ax, ayl, unit, n):
        start = (ax * 4 + ayl * 2 + c) * WROWS + unit * UNIT
        return full.at[pl.ds(pl.multiple_of(start, UNIT), n * UNIT)]

    own_in = load(w_ref, rows(x, yl, 0, 4))
    pl.semaphore_wait(barrier, len(peers))

    sent = []
    waited = []

    def copy_of(src, dst, to):
        i = len(sent)
        copy = pltpu.make_async_remote_copy(
            src_ref=src,
            dst_ref=dst,
            send_sem=ssem.at[i],
            recv_sem=rsem.at[i],
            device_id=to,
            device_id_type=MESH,
        )
        sent.append(copy)
        return copy

    def send(src, dst, to):
        copy = copy_of(src, dst, to)
        copy.start()
        return copy

    def landed(*copies):
        for copy in copies:
            if not any(copy is done for done in waited):
                waited.append(copy)
                copy.wait_recv()

    def mine(unit, n):
        return w_ref.at[pl.ds(unit * UNIT, n * UNIT)]

    def pages(az, rel, p):
        half = h if rel == 0 else 1 - h
        return moved.at[pl.ds(CROSS_AT + az * QPAGES + half * HPAGES + p, 1)]

    def relay(ref, to):
        return send(ref, ref, to)

    a1 = [send(mine(0, 2), rows(x, yl, 0, 2), to) for to in (to_xp, to_xm)]
    b1 = [send(mine(2, 1), rows(x, yl, 2, 1), to_s), send(mine(3, 1), rows(x, yl, 3, 1), to_c)]

    slot = group * REQ_DEV + z
    request = lax.fori_loop(
        0, NREQ, lambda i, found: jnp.where(slots[i] == slot, i, found), jnp.int32(0)
    )
    length = lens[request]
    base = group * REQ_DEV
    to_chip, to_cross = base, base
    for i in range(REQ_DEV):
        aim = slots[base + i] // REQ_DEV
        to_chip = jnp.where(aim == partner, base + i, to_chip)
        to_cross = jnp.where(aim == across, base + i, to_cross)

    pool_in.wait()
    first = z * QPAGES + h * HPAGES
    for p in range(HPAGES):
        cross_out[p] = store[table[to_cross, first + p]]

    def pick(p, carry):
        chip_out[p] = store[table[to_chip, p]]
        return carry

    lax.fori_loop(0, MAXP, pick, 0)

    tokens_in.wait()
    inputs = tokens[...].astype(F32)
    normed[...] = (inputs * rms(inputs) * in_gain[...]).astype(BF16)

    crossing = [
        send(cross_out.at[pl.ds(p, 1)], moved.at[pl.ds(CROSS_AT + first + p, 1)], to_t[rel])
        for p in range(HPAGES)
        for rel in range(2)
    ]
    b2 = [send(mine(2, 2), rows(x, yl, 2, 2), to) for to in (to_xp, to_xm)]
    a3 = [[send(mine(0, 1), rows(x, yl, 0, 1), to_s), send(mine(1, 1), rows(x, yl, 1, 1), to_c)]]
    chip_copy = send(chip_out, moved.at[pl.ds(0, MAXP)], to_p)
    rest = [send(w_ref, rows(x, yl, 0, 4), to_p)]

    position = (length + h * ROWS + lax.broadcasted_iota(jnp.int32, (ROWS, 1), 0)).astype(F32)
    angle = position * inverse[...]
    cosine[...] = jnp.cos(angle)
    sine[...] = jnp.sin(angle)

    wkv_in.wait()
    for g in range(KVH):
        k0, v0, end = 2 * g * HD, (2 * g + 1) * HD, (2 * g + 2) * HD
        key = dot(normed[...], wkv[:, k0:v0])
        key = rotated(key * rms(key) * k_gain[...], cosine[...], sine[...])
        kv[:, k0:v0] = key.astype(BF16)
        value = dot(normed[...], wkv[:, v0:end])
        kv[:, v0:end] = (value * rms(value)).astype(BF16)

    landed(*a1)
    a2 = [relay(rows(xm, yl, 0, 1), to_xp), relay(rows(xp, yl, 1, 1), to_xm)]
    for ax in (xm, xp):
        a3.append([relay(rows(ax, yl, 0, 1), to_s), relay(rows(ax, yl, 1, 1), to_c)])
        rest.append(relay(rows(ax, yl, 0, 2), to_p))

    kv_copy = copy_of(kv, other, to_o)

    @pl.when(h == 0)
    def _():
        kv_copy.start()
        other[...] = jnp.zeros_like(other)

    landed(*b1)
    b2y = [relay(rows(x, ol, 2, 2), to) for to in (to_xp, to_xm)]
    rest.append(relay(rows(x, ol, 2, 2), to_p))

    def heads(i):
        wq_in[i].wait()

        def head(j, carry):
            n = 2 * i + j
            raw = dot(normed[...], wq[:, pl.ds(pl.multiple_of(n * HD, HD), HD)])
            raw = rotated(raw * rms(raw) * q_gain[...], cosine[...], sine[...])
            query[n] = raw.astype(BF16) * BF16(HD**-0.5)
            return carry

        lax.fori_loop(0, 2, head, 0)

    ring = []
    ends = [chip_copy]

    def ring_step(p):
        for rel in range(2):
            landed(crossing[2 * p + rel])
            for to in (to_zp, to_zm):
                ring.append(relay(pages(z, rel, p), to))

    def ring_next(p):
        for rel in range(2):
            landed(ring[4 * p + 2 * rel], ring[4 * p + 2 * rel + 1])
            ends.append(relay(pages(zm, 0, p), to_zp) if rel == 0 else relay(pages(zp, 1, p), to_zm))

    heads(0)
    ring_step(0)
    heads(1)
    ring_step(1)
    heads(2)
    landed(*b2)
    b3 = [relay(rows(xm, yl, 2, 1), to_xp), relay(rows(xp, yl, 3, 1), to_xm)]
    for ax in (xm, xp):
        rest.append(relay(rows(ax, yl, 2, 2), to_p))
    heads(3)
    ring_next(0)

    low = contract(normed[...], left_t[...]).astype(BF16)
    u = dot(low, right[...])
    laurel = normed[...].astype(F32) + u * rms(u) * l_gain[...]
    side[...] = tokens[...].astype(F32) + laurel
    ring_next(1)

    causal = lax.broadcasted_iota(jnp.int32, (ROWS, ROWS), 1) <= lax.broadcasted_iota(
        jnp.int32, (ROWS, ROWS), 0
    )

    def fresh_heads(g):
        k0, v0, end = 2 * g * HD, (2 * g + 1) * HD, (2 * g + 2) * HD

        def head(i, carry):
            n = g * PER_KV + i
            q = query[n]
            now = jnp.where(causal, contract(q, kv[:, k0:v0]), -jnp.inf)
            past = jnp.where(h == 1, contract(q, other[:, k0:v0]), -jnp.inf)
            top = jnp.maximum(jnp.max(now, axis=-1, keepdims=True), jnp.max(past, axis=-1, keepdims=True))
            now, past = jnp.exp(now - top), jnp.exp(past - top)
            tops[n] = top
            totals[n] = jnp.sum(now, axis=-1, keepdims=True) + jnp.sum(past, axis=-1, keepdims=True)
            sums[n] = dot(now.astype(BF16), kv[:, v0:end]) + dot(past.astype(BF16), other[:, v0:end])
            return carry

        lax.fori_loop(0, PER_KV, head, 0)

    @pl.when(h == 1)
    def _():
        kv_copy.wait_recv()

    waited.append(kv_copy)
    fresh_heads(0)
    landed(*a2)
    a3.append([relay(rows(x2, yl, 0, 1), to_s), relay(rows(x2, yl, 1, 1), to_c)])
    rest.append(relay(rows(x2, yl, 0, 2), to_p))
    landed(*b2y)
    b3 += [relay(rows(xm, ol, 2, 1), to_xp), relay(rows(xp, ol, 3, 1), to_xm)]
    for ax in (xm, xp):
        rest.append(relay(rows(ax, ol, 2, 2), to_p))
    fresh_heads(1)

    for ax, pair in zip((x, xm, xp), a3[:3]):
        landed(*pair)
        rest.append(relay(rows(ax, ol, 0, 2), to_p))
    landed(*ends)
    home = request // REQ_DEV
    local = home == group
    shift = jnp.where(home == partner, 0, CROSS_AT)

    def settle(p, carry):
        cache[pl.ds(pl.multiple_of(p * PAGE, PAGE), PAGE)] = jnp.where(
            local, store[table[request, p]], moved[shift + p]
        )
        return carry

    lax.fori_loop(0, MAXP, settle, 0)
    seen = lax.broadcasted_iota(jnp.int32, (1, LMAX), 1) < length

    def cached_heads(g):
        k0, v0, end = 2 * g * HD, (2 * g + 1) * HD, (2 * g + 2) * HD

        def head(i, carry):
            n = g * PER_KV + i
            scores = jnp.where(seen, contract(query[n], cache[:, k0:v0]), -jnp.inf)
            top = jnp.maximum(tops[n], jnp.max(scores, axis=-1, keepdims=True))
            keep = jnp.exp(tops[n] - top)
            scores = jnp.exp(scores - top)
            total = totals[n] * keep + jnp.sum(scores, axis=-1, keepdims=True)
            result = sums[n] * keep + dot(scores.astype(BF16), cache[:, v0:end])
            attended[:, pl.ds(pl.multiple_of(n * HD, HD), HD)] = (result / total).astype(BF16)
            return carry

        lax.fori_loop(0, PER_KV, head, 0)

    cached_heads(0)
    landed(*b3)
    rest.append(relay(rows(x2, yl, 2, 2), to_p))
    rest.append(relay(rows(x2, ol, 2, 2), to_p))
    landed(*a3[3])
    rest.append(relay(rows(x2, ol, 0, 2), to_p))
    cached_heads(1)
    for copy in loads[-1:]:
        copy.wait()
    landed(*rest)

    def column(i, square):
        part = dot(attended[...], full[:, pl.ds(pl.multiple_of(i * HD, HD), HD)])
        projected[:, pl.ds(pl.multiple_of(i * HD, HD), HD)] = part
        return square + jnp.sum(part * part, axis=-1, keepdims=True)

    square = lax.fori_loop(0, D // HD, column, jnp.zeros((ROWS, 1), F32))
    scale = lax.rsqrt(square / D + EPS)
    attn = projected[...] * scale * p_gain[...]
    mixed[...] = ((attn + side[...]) / math.sqrt(2.0)).astype(BF16)
    landed(*sent)
    for copy in sent:
        if copy is not kv_copy:
            copy.wait_send()

    @pl.when(h == 0)
    def _():
        kv_copy.wait_send()


def shards(
    tokens, input_gain, w_query, w_keyval, query_gain, key_gain, w_output, laurel_left,
    laurel_right, laurel_gain, post_gain, cache_pool, page_table, cached_len, slot_of,
):
    smem = pl.BlockSpec(memory_space=pltpu.SMEM)
    vmem = pl.BlockSpec(memory_space=pltpu.VMEM)
    stay = pl.BlockSpec(memory_space=pl.ANY)
    return pl.pallas_call(
        block_kernel,
        out_shape=jax.ShapeDtypeStruct((ROWS, D), BF16),
        in_specs=[smem] * 3 + [vmem] * 8 + [stay] * 5,
        out_specs=vmem,
        scratch_shapes=[
            pltpu.VMEM((ROWS, D), BF16),
            pltpu.VMEM((D, NH * HD), BF16),
            pltpu.VMEM((D, KVW), BF16),
            pltpu.VMEM((D, D), BF16),
            pltpu.VMEM((POOL, PAGE, KVW), BF16),
            pltpu.VMEM((2 * MAXP, PAGE, KVW), BF16),
            pltpu.VMEM((MAXP, PAGE, KVW), BF16),
            pltpu.VMEM((HPAGES, PAGE, KVW), BF16),
            pltpu.VMEM((LMAX, KVW), BF16),
            pltpu.VMEM((ROWS, D), BF16),
            pltpu.VMEM((ROWS, HALF), F32),
            pltpu.VMEM((ROWS, HALF), F32),
            pltpu.VMEM((NH, ROWS, HD), BF16),
            pltpu.VMEM((ROWS, KVW), BF16),
            pltpu.VMEM((ROWS, KVW), BF16),
            pltpu.VMEM((ROWS, D), F32),
            pltpu.VMEM((ROWS, D), BF16),
            pltpu.VMEM((ROWS, D), F32),
            pltpu.VMEM((NH, ROWS, 1), F32),
            pltpu.VMEM((NH, ROWS, 1), F32),
            pltpu.VMEM((NH, ROWS, HD), F32),
            pltpu.SemaphoreType.DMA((N_COPIES,)),
            pltpu.SemaphoreType.DMA((N_COPIES,)),
            pltpu.SemaphoreType.DMA((16,)),
        ],
        compiler_params=pltpu.CompilerParams(
            collective_id=0, has_side_effects=True, vmem_limit_bytes=VMEM_LIMIT
        ),
        name="block",
    )(
        page_table, cached_len, slot_of,
        input_gain[None], query_gain[None], key_gain[None], laurel_left.T, laurel_right,
        laurel_gain[None], post_gain[None], jnp.asarray(INVERSE),
        tokens, w_query, w_keyval, w_output, cache_pool,
    )


def solution(mesh):
    in_specs = (
        P(("req", "head"), None),
        P(), P(), P(), P(), P(),
        P("req", None),
        P(), P(), P(), P(),
        P("req", None, None),
        P(), P(), P(),
    )
    out_specs = P(("req", "head"), None)
    return jax.shard_map(shards, mesh=mesh, in_specs=in_specs, out_specs=out_specs, check_vma=False)
```

time: 261 us -> 60.5 us (0.23)
  the two profiles are of different devices: /device:TPU:1 before, /device:TPU:16 now
where the time goes in v2:
time: 60.5 us; the launch traced here: 60.2 us
  Pallas kernels  56.5 us (93%)
  local copies, waits for them, and re-layouts  3.7 us (6%)
    pallas_call x1, Pallas kernels, shards(): pl.pallas_call(block_kernel, out_shape=jax.ShapeDtypeStruct((ROWS, D), BF...  56.5 us
    unnamed x2, local copies, waits for them, and re-layouts  3.7 us

profile of v2, /device:TPU:16, one launch (start us, length us, event | category | flops | bytes accessed | tf_op | source)
XLA Modules:
  0.0 60.2 jit_solution(4627036551887017296)
XLA Ops:
  0.0 1.4 %copy.17.table = s32[64,16]{1,0:T(8,128)} copy(s32[64,16]{0,1:T(8,128)} %param.28) | data formatting | bytes 8192 | tf_op args[12]
  1.4 56.5 %block.1 = bf16[256,2048]{1,0:T(8,128)(2,1)} custom-call(s32[64,16]{1,0:T(8,128)} %copy.17.table, s32[64]{0:T(128)} %lens.1, s32[64]{0:T(128)} %slots.1, f32[1,2048]{1,0:T(1,128)} %bitcast.7, f32[1,256]{1,0:T(1,128)} %bitcast.10, f32[1,256]{1,0:T(1,128)} %bitcast.11, bf16[64,2048]{1,0:T(8,128)(2,1)} %bitcast.6, bf16[64,2048]{1,0:T(8,128)(2,1)} %right.1, ...), custom_call_target="tpu_custom_call" | custom-call | tf_op jit(solution)/shard_map/block/pallas_call | solution.py:372
  57.9 2.3 %copy.19 = bf16[256,2048]{1,0:T(8,128)(2,1)} copy(bf16[256,2048]{1,0:T(8,128)(2,1)} %block.1) | data formatting | bytes 2097152
